TPU v7x, 256 devices: a whole 4x4x8 slice. The times are simulated.
256 devices in a mesh: space: 32 (over z_lo, y, core), snap: 8 (over z_hi, x).
Axes of the slice: x: 4, y: 4, z: 8 (z_hi: 2, z_lo: 4; z = z_hi * 4 + z_lo), core: 2. Of those that a mesh axis runs over, the one named last changes fastest.
Arguments:
- forcing_direct: bfloat16 [1024, 32, 16, 128], P('snap', 'space'), may hold values from -6 to 6
- forcing_adjoint: bfloat16 [1024, 32, 16, 128], P('snap', 'space'), may hold values from -6 to 6
- conductance: float32 [32, 16, 128], P('space'), may hold values from 0.25 to 4
- shift_table: float32 [16], replicated, may hold values from 0.2 to 3
- freq_direct: int32 [1024], P('snap'), may hold values from 0 to 15
- freq_adjoint: int32 [1024], P('snap'), may hold values from 0 to 15
- left_factors: float32 [1024, 64], replicated, may hold values from -0.1875 to 0.1875
- right_factors: float32 [1024, 64], replicated, may hold values from -0.1875 to 0.1875
- singular_values: float32 [64], replicated, may hold values from 0.25 to 4
Outputs:
- gram: float32 [1024, 1024], P('snap', 'space')
- direct_modes: float32 [64, 32, 16, 128], P(None, 'space', 'snap')
- adjoint_modes: float32 [64, 32, 16, 128], P(None, 'space', 'snap')
All inputs are finite; a program needn't handle non-finite values.
Results may differ from a plain program's by a relative error of at most 0.0041.
Values may be sent and summed in bfloat16 or wider, within the bound.
A program may use at most 64 MiB of HBM per device.

v0:
```python
import math

import jax
import jax.numpy as jnp
from jax import lax
from jax.sharding import PartitionSpec as P


def extended(cells, sides, width):
    for axis, dim in sides:
        count = lax.axis_size(axis)
        ends = count - 1
        head = lax.slice_in_dim(cells, 0, width, axis=dim)
        tail = lax.slice_in_dim(cells, cells.shape[dim] - width, cells.shape[dim], axis=dim)
        cells = jnp.concatenate(
            [
                lax.ppermute(tail, axis, [(i, (i + 1) % count) for i in range(ends)]),
                cells,
                lax.ppermute(head, axis, [((i + 1) % count, i) for i in range(ends)]),
            ],
            axis=dim,
        )
    return cells


def lookup(indices, shift_list):
    levels = jnp.arange(shift_list.shape[0], dtype=jnp.int32)
    picked = jnp.where(indices[:, None] == levels[None, :], shift_list[None, :], jnp.float32(0.0))
    return jnp.sum(picked, axis=1)


def shifted_sum(values, axis):
    length = values.shape[axis]
    upper = lax.slice_in_dim(values, 1, length, axis=axis)
    lower = lax.slice_in_dim(values, 0, length - 1, axis=axis)
    edge_shape = list(values.shape)
    edge_shape[axis] = 1
    edge = jnp.zeros(edge_shape, values.dtype)
    return jnp.concatenate([upper, edge], axis=axis) + jnp.concatenate([edge, lower], axis=axis)


def neighbours(padded):
    middle = padded[:, :, 1:-1]
    summed = padded[:, :, 2:] + padded[:, :, :-2]
    return summed + shifted_sum(middle, 3) + shifted_sum(middle, 4)


def per_device(
    forcing_direct,
    forcing_adjoint,
    conductance,
    shift_table,
    freq_direct,
    freq_adjoint,
    left_factors,
    right_factors,
    singular_values,
):
    n_space = lax.axis_size("space")
    n_snap = lax.axis_size("snap")
    rows_dev = forcing_direct.shape[0]
    plane_x = forcing_direct.shape[1]
    width_y = forcing_direct.shape[2]
    width_z = forcing_direct.shape[3]
    total_snaps = rows_dev * n_snap
    weight = 1.0 / math.sqrt(plane_x * n_space * width_y * width_z)
    shifts = jnp.stack([lookup(freq_direct, shift_table), lookup(freq_adjoint, shift_table)])
    diagonal = shifts[:, :, None, None, None] + 6.0 * conductance[None, None]
    forcing = jnp.stack([forcing_direct, forcing_adjoint])
    unit_field = jnp.ones_like(conductance)
    send_scale = jnp.stack([unit_field, conductance])[:, None]
    take_scale = jnp.stack([conductance, unit_field])[:, None]
    state = forcing.astype(jnp.float32) / diagonal
    for repeat in range(2):
        padded = extended(state * send_scale, (("space", 2),), 1)
        state = (forcing.astype(jnp.float32) + take_scale * neighbours(padded)) / diagonal
    snapshots = state.astype(jnp.bfloat16)
    inv_root = 1.0 / jnp.sqrt(singular_values)
    right_scaled = (right_factors * inv_root[None, :]).astype(jnp.bfloat16)
    left_scaled = (left_factors * inv_root[None, :]).astype(jnp.bfloat16)
    exchanged = lax.all_to_all(snapshots, "snap", split_axis=3, concat_axis=1, tiled=True)
    local_y = exchanged.shape[3]
    flattened = exchanged.reshape(2, total_snaps, -1)
    column_width = total_snaps // n_space
    adjoint_blocks = flattened[1].reshape(n_snap, rows_dev, -1)
    direct_blocks = flattened[0].reshape(n_space, column_width, -1)
    partial_terms = jnp.einsum(
        "iak,jbk->jiab", adjoint_blocks, direct_blocks, preferred_element_type=jnp.float32
    )
    partial_terms = partial_terms.reshape(n_space * n_snap * rows_dev, column_width)
    gram = (
        lax.psum_scatter(partial_terms, ("space", "snap"), scatter_dimension=0, tiled=True) * weight
    )
    direct_modes = jnp.einsum(
        "br,bk->rk", right_scaled, flattened[0], preferred_element_type=jnp.float32
    )
    adjoint_modes = jnp.einsum(
        "br,bk->rk", left_scaled, flattened[1], preferred_element_type=jnp.float32
    )
    direct_modes = direct_modes.reshape(-1, plane_x, local_y, width_z)
    adjoint_modes = adjoint_modes.reshape(-1, plane_x, local_y, width_z)
    return (gram, direct_modes, adjoint_modes)


def solution(mesh):
    placed = (
        P("snap", "space", None, None),
        P("snap", "space", None, None),
        P("space", None, None),
        P(),
        P("snap"),
        P("snap"),
        P(),
        P(),
        P(),
    )
    return jax.shard_map(
        per_device,
        mesh=mesh,
        in_specs=placed,
        out_specs=(
            P("snap", "space"),
            P(None, "space", "snap", None),
            P(None, "space", "snap", None),
        ),
        check_vma=False,
    )
```

profile of v0, /device:TPU:32, one launch (start us, length us, event | category | flops | bytes accessed | tf_op | source)
XLA Modules:
  0.0 1636.3 jit_solution(16273075380002994177)
XLA Ops:
  7.2 0.0 reduce-scatter.2.cloned.1.call-start
  7.2 0.7 multiply_bitcast_fusion
  7.9 0.8 pad_bitcast_fusion.1
  8.7 0.8 select_reduce_fusion.1
  9.5 1.5 copy_bitcast_fusion.4
  11.0 0.5 fusion
  11.4 1.9 collective-permute-start.1
  13.4 5.8 collective-permute-start
  19.2 0.5 fusion.12
  19.6 0.7 fusion.13
  20.4 20.5 %collective-permute-done.1 = f32[2,128,1,16,128]{4,1,2,0,3:T(8,128)S(1)} collective-permute-done((f32[2,128,1,16,128]{4,1,2,0,3:T(8,128)S(1)}, f32[2,128,1,16,128]{4,1,2,0,3:T(8,128)S(1)}, u32[]{:S(2)}, u32[]{:S(2)}) %collective-permute-start.1) | collective-permute-done | bytes 2097184 | tf_op jit(solution)/shard_map/ppermute | solution.py:17
  40.9 1.8 collective-permute-done
  42.7 1.6 fusion.1
  44.3 1.9 collective-permute-start.3
  46.2 5.9 collective-permute-start.2
  52.1 0.5 fusion.10
  52.6 0.8 fusion.11
  53.4 20.5 %collective-permute-done.3 = f32[2,128,1,16,128]{4,1,2,0,3:T(8,128)S(1)} collective-permute-done((f32[2,128,1,16,128]{4,1,2,0,3:T(8,128)S(1)}, f32[2,128,1,16,128]{4,1,2,0,3:T(8,128)S(1)}, u32[]{:S(2)}, u32[]{:S(2)}) %collective-permute-start.3) | collective-permute-done | bytes 2097184 | tf_op jit(solution)/shard_map/ppermute | solution.py:17
  73.9 1.8 collective-permute-done.2
  75.7 1.5 fusion.2
  77.1 38.7 %all_to_all.15 = bf16[2,128,1,16,128]{4,1,2,0,3:T(8,128)(2,1)S(1)} all-to-all(bf16[2,128,1,16,128]{4,1,2,0,3:T(8,128)(2,1)S(1)} %fusion.2), channel_id=1, replica_groups=mesh['space'=32,'snap'=8] {'snap'}, dimensions={3} | all-to-all | bytes 2097152 | tf_op jit(solution)/shard_map/all_to_all | solution.py:81
  115.8 1.1 copy.54
  116.9 0.8 fusion.14
  117.7 0.3 reshape.122
  118.0 0.3 reshape.123
  118.4 0.7 convolution_bitcast_fusion
  119.1 2.4 copy.38
  121.6 4.4 copy.53
  126.0 0.0 copy-start.2
  126.0 0.0 reduce-scatter.2.cloned.1.call-update
  126.0 0.6 copy-done.2
  126.6 0.0 copy-start
  126.6 0.1 copy.55
  126.7 0.0 copy-start.1
  126.7 0.2 copy.40
  126.9 0.6 copy-done
  127.6 0.3 convolution_bitcast_fusion.1
  127.8 0.7 copy.42
  128.5 0.1 copy.56
  128.6 0.2 copy.39
  128.8 0.0 copy-done.1
  128.8 0.3 convolution_bitcast_fusion.2
  129.1 0.7 copy.41
  129.8 1498.3 %reduce-scatter.2.cloned.1.call-done = f32[128,32]{0,1:T(8,128)} async-done(((f32[32768,32]{0,1:T(8,128)}), f32[128,32]{0,1:T(8,128)}) %reduce-scatter.2.cloned.1.call-update) | async-done | bytes 16400 | tf_op jit(solution)/shard_map/reduce_scatter | solution.py:92
  1628.1 1.3 broadcast_multiply_fusion
  (4 shorter events, 0.0 us)
Async XLA Ops:
  7.2 1620.9 %reduce-scatter.2.cloned.1.call-start = ((), (), s32[]{:S(2)}) async-start(), calls=%async_computation.2 | async-start | bytes 4210688 | tf_op jit(solution)/shard_map/reduce_scatter | solution.py:92
  11.4 29.5 %collective-permute-start.1 = (f32[2,128,1,16,128]{4,1,2,0,3:T(8,128)S(1)}, f32[2,128,1,16,128]{4,1,2,0,3:T(8,128)S(1)}, u32[]{:S(2)}, u32[]{:S(2)}) collective-permute-start(f32[2,128,1,16,128]{4,1,2,0,3:T(8,128)S(1)} %fusion), channel_id=1, source_target_pairs={{0,8},{8,16},{16,24},{24,32},{32,40},{40,48},{48,56},{56,64},{64,7... | collective-permute-start | bytes 6291464 | tf_op jit(solution)/shard_map/ppermute | solution.py:17
  13.4 29.3 %collective-permute-start = (f32[2,128,1,16,128]{4,1,2,0,3:T(8,128)S(1)}, f32[2,128,1,16,128]{4,1,2,0,3:T(8,128)S(1)}, u32[]{:S(2)}, u32[]{:S(2)}) collective-permute-start(f32[2,128,1,16,128]{4,1,2,0,3:T(8,128)S(1)} %fusion), channel_id=1, source_target_pairs={{8,0},{16,8},{24,16},{32,24},{40,32},{48,40},{56,48},{64,56},{72,6... | collective-permute-start | bytes 6291464 | tf_op jit(solution)/shard_map/ppermute | solution.py:19
  44.3 29.6 %collective-permute-start.3 = (f32[2,128,1,16,128]{4,1,2,0,3:T(8,128)S(1)}, f32[2,128,1,16,128]{4,1,2,0,3:T(8,128)S(1)}, u32[]{:S(2)}, u32[]{:S(2)}) collective-permute-start(f32[2,128,1,16,128]{4,1,2,0,3:T(8,128)S(1)} %fusion.1), channel_id=1, source_target_pairs={{0,8},{8,16},{16,24},{24,32},{32,40},{40,48},{48,56},{56,64},{64,7... | collective-permute-start | bytes 6291464 | tf_op jit(solution)/shard_map/ppermute | solution.py:17
  46.2 29.5 %collective-permute-start.2 = (f32[2,128,1,16,128]{4,1,2,0,3:T(8,128)S(1)}, f32[2,128,1,16,128]{4,1,2,0,3:T(8,128)S(1)}, u32[]{:S(2)}, u32[]{:S(2)}) collective-permute-start(f32[2,128,1,16,128]{4,1,2,0,3:T(8,128)S(1)} %fusion.1), channel_id=1, source_target_pairs={{8,0},{16,8},{24,16},{32,24},{40,32},{48,40},{56,48},{64,56},{72,6... | collective-permute-start | bytes 6291464 | tf_op jit(solution)/shard_map/ppermute | solution.py:19
  126.0 0.7 copy-start.2
  126.6 0.9 copy-start
  126.7 2.1 copy-start.1
Sparse Core Ops, SparseCore 0:
  126.1 1501.9 reduce-scatter.1
where the time goes:
time: 1640 us
  waiting for transfers between devices  1540 us (94%)
  blocking collectives  38.7 us (2%)
  local copies, waits for them, and re-layouts  17.2 us (1%)
    reduce_scatter x1, waiting for transfers between devices, per_device(): lax.psum_scatter(partial_terms, ('space', 'snap'), scatter_dimension=0, t...  1500 us
    ppermute x2, waiting for transfers between devices, extended(): lax.ppermute(tail, axis, [(i, (i + 1) % count) for i in range(ends)])  41.1 us
    all_to_all x1, blocking collectives, per_device(): lax.all_to_all(snapshots, 'snap', split_axis=3, concat_axis=1, tiled=True)  38.7 us
  transfers between devices with their start and end apart: 5, of which 5 were waited for; matrix products, arithmetic and copies ran while one was open for 0% of the time, Pallas kernels for 0%

commit v1 on v0

v1 whole, which is shorter than its diff:
```python
import functools
import math

import jax
import jax.numpy as jnp
from jax import lax
from jax.experimental import pallas as pl
from jax.experimental.pallas import tpu as pltpu
from jax.sharding import PartitionSpec as P

MESH = pl.DeviceIdType.MESH
F32 = jnp.float32
BF16 = jnp.bfloat16

ROWS = 16
LANES = 128
PLANES = 6
PART = 32
LEVELS = 16


def contract_last(a, b):
    return lax.dot_general(a, b, (((1,), (1,)), ((), ())), preferred_element_type=F32)


def contract_first(a, b):
    return lax.dot_general(a, b, (((0,), (0,)), ((), ())), preferred_element_type=F32)


def kernel(
    weight,
    fd, fa, cond, table, freq_d, freq_a, left, right, sing,
    gram_o, dm_o, am_o,
    field, chalo, rtab, crtab, turn, outbox, dirbox, adjbox,
    psend, precv, gsum, bsend, brecv, mpart, mrecv, lbuf, rbuf,
    halo_s, halo_r, cond_s, cond_r, load_s, post_s, post_r, sa_s, sa_r, sb_s, sb_r, md_s, md_r,
):
    s = lax.axis_index("space")
    p = lax.axis_index("snap")
    j, h = s // 2, s % 2
    zl, y = j // 4, j % 4
    zh, x = p // 4, p % 4
    forcing = (fd, fa)

    def dev(ss, pp):
        return (ss, pp)

    barrier = pltpu.get_barrier_semaphore()
    greet = [dev(2 * j + 1 - h, p)]
    for dj in (-1, 1):
        for dh in (0, 1):
            greet.append(dev(2 * ((j + dj + 16) % 16) + dh, p))
    for dz in range(2):
        for dx in range(4):
            if dz or dx:
                greet.append(dev(s, ((zh + dz) % 2) * 4 + (x + dx) % 4))
    for dx in range(1, 4):
        greet.append(dev(2 * j + 1 - h, zh * 4 + (x + dx) % 4))
    for dy in range(1, 4):
        for dx in range(4):
            greet.append(dev(2 * (zl * 4 + (y + dy) % 4) + h, zh * 4 + (x + dx) % 4))
    for dz in range(1, 4):
        greet.append(dev(2 * (((zl + dz) % 4) * 4 + y) + h, p))
    for target in greet:
        pl.semaphore_signal(barrier, inc=1, device_id=target, device_id_type=MESH)
    pl.semaphore_wait(barrier, len(greet))

    def start_row(fam, part, half):
        return part * 64 + half * 32 if fam == 0 else half * 64 + part * 32

    def halo_copy(c, dj, half):
        fam, part = c // 2, c % 2
        slot = 2 * (dj + 1)
        return pltpu.make_async_remote_copy(
            src_ref=forcing[fam].at[pl.ds(start_row(fam, part, half), PART)],
            dst_ref=field.at[fam, part, 2 * (1 - dj) + h],
            send_sem=halo_s.at[c, slot + half],
            recv_sem=halo_r.at[c, 2 * (1 - dj) + h],
            device_id=dev(2 * (j + dj) + half, p),
            device_id_type=MESH,
        )

    def halo_own(c):
        fam, part = c // 2, c % 2
        return pltpu.make_async_copy(
            forcing[fam].at[pl.ds(start_row(fam, part, h), PART)],
            field.at[fam, part, 2 + h],
            load_s.at[c],
        )

    def cond_copy(dj, half):
        return pltpu.make_async_remote_copy(
            src_ref=cond,
            dst_ref=chalo.at[2 * (1 - dj) + h],
            send_sem=cond_s.at[2 * (dj + 1) + half],
            recv_sem=cond_r.at[2 * (1 - dj) + h],
            device_id=dev(2 * (j + dj) + half, p),
            device_id_type=MESH,
        )

    def to_neighbours(act):
        for dj, inside in ((1, j < 15), (-1, j > 0)):
            @pl.when(inside)
            def _():
                for half in range(2):
                    act(dj, half)
        act(0, 1 - h)

    def from_neighbours(act):
        for dj, inside in ((-1, j > 0), (1, j < 15)):
            @pl.when(inside)
            def _():
                for half in range(2):
                    act(dj, half)
        act(0, 1 - h)

    to_neighbours(lambda dj, half: cond_copy(dj, half).start())
    for c in range(4):
        to_neighbours(lambda dj, half: halo_copy(c, dj, half).start())
        halo_own(c).start()
    lcopy = pltpu.make_async_copy(left.at[pl.ds(zh * 4, 4)], lbuf, load_s.at[4])
    rcopy = pltpu.make_async_copy(right.at[:, :, h], rbuf, load_s.at[5])
    ccopy = pltpu.make_async_copy(cond, chalo.at[2 + h], load_s.at[6])
    lcopy.start()
    rcopy.start()
    ccopy.start()

    for first, edge in ((0, j == 0), (4, j == 15)):
        @pl.when(edge)
        def _():
            for k in range(2):
                chalo[first + k] = jnp.ones((ROWS, LANES), F32)
                for fam in range(2):
                    for part in range(2):
                        field[fam, part, first + k] = jnp.zeros((PART, ROWS, LANES), BF16)

    def cond_arrival(dj, half):
        pltpu.make_async_remote_copy(
            src_ref=cond,
            dst_ref=chalo.at[2 * (1 + dj) + half],
            send_sem=cond_s.at[0],
            recv_sem=cond_r.at[2 * (1 + dj) + half],
            device_id=dev(s, p),
            device_id_type=MESH,
        ).wait_recv()

    def halo_arrival(c):
        fam, part = c // 2, c % 2

        def act(dj, half):
            pltpu.make_async_remote_copy(
                src_ref=forcing[fam].at[pl.ds(0, PART)],
                dst_ref=field.at[fam, part, 2 * (1 + dj) + half],
                send_sem=halo_s.at[c, 0],
                recv_sem=halo_r.at[c, 2 * (1 + dj) + half],
                device_id=dev(s, p),
                device_id_type=MESH,
            ).wait_recv()

        return act

    ccopy.wait()
    from_neighbours(cond_arrival)

    def fill(level, carry):
        shift = table[level]
        for q in range(PLANES):
            there = j + (q // 2 - 1)
            mask = jnp.where((there >= 0) & (there < 16), F32(1.0), F32(0.0))
            coeff = chalo[q]
            inverse = mask / (shift + 6.0 * coeff)
            rtab[level, q] = inverse
            crtab[level, q] = coeff * inverse
        return carry

    lax.fori_loop(0, LEVELS, fill, 0)

    row = lax.broadcasted_iota(jnp.int32, (ROWS, LANES), 0)
    lane = lax.broadcasted_iota(jnp.int32, (ROWS, LANES), 1)

    def flat_sum(v):
        up = jnp.where(row == 0, 0.0, pltpu.roll(v, 1, 0))
        down = jnp.where(row == ROWS - 1, 0.0, pltpu.roll(v, ROWS - 1, 0))
        fore = jnp.where(lane == 0, 0.0, pltpu.roll(v, 1, 1))
        aft = jnp.where(lane == LANES - 1, 0.0, pltpu.roll(v, LANES - 1, 1))
        return (up + down) + (fore + aft)

    def smooth(fam, part):
        freq = freq_d if fam == 0 else freq_a
        base = start_row(fam, part, h)

        def one(n, carry):
            level = freq[base + n]
            f = [field[fam, part, q, n].astype(F32) for q in range(PLANES)]
            if fam == 0:
                r = [rtab[level, q] for q in range(PLANES)]
                g = [crtab[level, q] for q in range(1, 5)]
                a0 = [f[q] * r[q] for q in range(PLANES)]
                a1 = [
                    a0[q] + g[q - 1] * (a0[q - 1] + a0[q + 1] + flat_sum(a0[q]))
                    for q in range(1, 5)
                ]
                a2 = [
                    a0[q] + g[q - 1] * (a1[q - 2] + a1[q] + flat_sum(a1[q - 1]))
                    for q in range(2, 4)
                ]
            else:
                g = [crtab[level, q] for q in range(PLANES)]
                r = [rtab[level, q] for q in range(2, 4)]
                a0 = [f[q] * g[q] for q in range(PLANES)]
                a1 = [
                    a0[q] + g[q] * (a0[q - 1] + a0[q + 1] + flat_sum(a0[q]))
                    for q in range(1, 5)
                ]
                a2 = [
                    (f[q] + (a1[q - 2] + a1[q] + flat_sum(a1[q - 1]))) * r[q - 2]
                    for q in range(2, 4)
                ]
            for k in range(2):
                turn[pl.ds(k * ROWS * PART + n, ROWS, stride=PART), :] = a2[k]
            return carry

        lax.fori_loop(0, PART, one, 0)

    def pack(c):
        for k in range(2):
            for yy in range(ROWS):
                owner = (yy % 8) // 2
                rho = k * 4 + (yy // 8) * 2 + yy % 2
                at = (k * ROWS + yy) * PART
                outbox[c, owner, rho] = turn[at : at + PART, :].astype(BF16)

    def post(c, dz, dx):
        part = c % 2
        to_x = (x + dx) % 4
        if c < 2:
            dst = dirbox.at[p, part]
            target = dev(s, ((zh + dz) % 2) * 4 + to_x)
        else:
            dst = adjbox.at[x, h, part]
            target = dev(2 * j + (h + dz) % 2, zh * 4 + to_x)
        src = outbox.at[c, to_x]
        if dz == 0 and dx == 0:
            return pltpu.make_async_copy(src, dst, post_r.at[c, 0])
        return pltpu.make_async_remote_copy(
            src_ref=src,
            dst_ref=dst,
            send_sem=post_s.at[c, dz * 4 + dx],
            recv_sem=post_r.at[c, dz * 4 + dx],
            device_id=target,
            device_id_type=MESH,
        )

    def post_arrival(c, dz, dx):
        part = c % 2
        from_x = (x + 4 - dx) % 4
        if c < 2:
            dst = dirbox.at[((zh + dz) % 2) * 4 + from_x, part]
        else:
            dst = adjbox.at[from_x, (h + dz) % 2, part]
        pltpu.make_async_remote_copy(
            src_ref=outbox.at[c, 0],
            dst_ref=dst,
            send_sem=post_s.at[c, 0],
            recv_sem=post_r.at[c, dz * 4 + dx],
            device_id=dev(s, p),
            device_id_type=MESH,
        ).wait_recv()

    far_first = [(dz, dx) for dz in (1, 0) for dx in (2, 1, 3, 0)]
    for c in range(4):
        halo_own(c).wait()
        from_neighbours(halo_arrival(c))
        smooth(c // 2, c % 2)
        pack(c)
        for dz, dx in far_first:
            post(c, dz, dx).start()

    lcopy.wait()
    rcopy.wait()
    inv_root = 1.0 / jnp.sqrt(sing[...])
    left_s = (lbuf[...].reshape(512, 64) * inv_root).astype(BF16)
    right_s = (rbuf[...].reshape(512, 64) * inv_root).astype(BF16)

    def arrived(c):
        for dz, dx in far_first:
            if dz == 0 and dx == 0:
                post(c, 0, 0).wait()
            else:
                post_arrival(c, dz, dx)

    for c in range(4):
        arrived(c)

    def adj_rows(xx):
        pieces = [
            jnp.concatenate([adjbox[xx, hh, part, rho] for rho in range(8)], axis=1)
            for hh in range(2)
            for part in range(2)
        ]
        return jnp.concatenate(pieces, axis=0)

    adj_all = [adj_rows((x + dx) % 4) for dx in range(4)]

    def sa_copy(dy, dx):
        return pltpu.make_async_remote_copy(
            src_ref=psend.at[dy * 4 + dx],
            dst_ref=precv.at[dy * 4 + dx],
            send_sem=sa_s.at[dy * 4 + dx],
            recv_sem=sa_r.at[dy * 4 + dx],
            device_id=dev(2 * (zl * 4 + (y + dy) % 4) + h, zh * 4 + (x + dx) % 4),
            device_id_type=MESH,
        )

    for dy in (2, 1, 3, 0):
        yy = (y + dy) % 4
        pieces = [
            jnp.concatenate([dirbox[2 * zz + yy // 2, yy % 2, rho] for rho in range(8)], axis=1)
            for zz in range(4)
        ]
        dir_y = jnp.concatenate(pieces, axis=0)
        for dx in (2, 1, 3, 0):
            block = contract_last(dir_y, adj_all[dx])
            if dy == 0 and dx == 0:
                gsum[...] = block
            else:
                psend[dy * 4 + dx] = block.astype(BF16)
                sa_copy(dy, dx).start()

    def dir_cells(k, t):
        rho = k * 4 + 2 * zh + t
        return jnp.concatenate(
            [dirbox[pp, part, rho] for pp in range(8) for part in range(2)], axis=0
        )

    def adj_cells(zz, t):
        rho = h * 4 + 2 * zz + t
        return jnp.concatenate(
            [adjbox[xx, hh, part, rho] for xx in range(4) for hh in range(2) for part in range(2)],
            axis=0,
        )

    for t in range(2):
        mpart[0, t] = contract_first(right_s, dir_cells(1 - h, t))
        mpart[1, t] = contract_first(left_s, adj_cells(1 - zh, t))

    def md_copy(fam):
        target = dev(2 * j + 1 - h, p) if fam == 0 else dev(s, (1 - zh) * 4 + x)
        return pltpu.make_async_remote_copy(
            src_ref=mpart.at[fam],
            dst_ref=mrecv.at[fam],
            send_sem=md_s.at[fam],
            recv_sem=md_r.at[fam],
            device_id=target,
            device_id_type=MESH,
        )

    for fam in range(2):
        md_copy(fam).start()
    own_d = [contract_first(right_s, dir_cells(h, t)) for t in range(2)]
    own_a = [contract_first(left_s, adj_cells(zh, t)) for t in range(2)]

    for dy in (1, 3, 2, 0):
        for dx in (1, 3, 2, 0):
            if dy or dx:
                sa_copy(dy, dx).wait_recv()
    total = gsum[...]
    for i in range(1, 16):
        total = total + precv[i].astype(F32)
    for zz in range(4):
        bsend[zz] = total[zz * 32 : zz * 32 + 32]

    def sb_copy(dz):
        return pltpu.make_async_remote_copy(
            src_ref=bsend.at[(zl + dz) % 4],
            dst_ref=brecv.at[dz],
            send_sem=sb_s.at[dz],
            recv_sem=sb_r.at[dz],
            device_id=dev(2 * (((zl + dz) % 4) * 4 + y) + h, p),
            device_id_type=MESH,
        )

    for dz in (2, 1, 3):
        sb_copy(dz).start()

    for fam in range(2):
        md_copy(fam).wait_recv()
    for t in range(2):
        dm_o[:, t, :] = own_d[t] + mrecv[0, t]
        am_o[:, t, :] = own_a[t] + mrecv[1, t]

    for dz in (1, 3, 2):
        sb_copy(dz).wait_recv()
    mine = bsend[zl] + brecv[1] + brecv[2] + brecv[3]
    gram_o[...] = (mine * weight).T

    to_neighbours(lambda dj, half: cond_copy(dj, half).wait_send())
    for c in range(4):
        to_neighbours(lambda dj, half: halo_copy(c, dj, half).wait_send())
        for dz, dx in far_first:
            if dz or dx:
                post(c, dz, dx).wait_send()
    for dy in range(4):
        for dx in range(4):
            if dy or dx:
                sa_copy(dy, dx).wait_send()
    for dz in range(1, 4):
        sb_copy(dz).wait_send()
    for fam in range(2):
        md_copy(fam).wait_send()


def per_device(
    forcing_direct,
    forcing_adjoint,
    conductance,
    shift_table,
    freq_direct,
    freq_adjoint,
    left_factors,
    right_factors,
    singular_values,
):
    weight = 1.0 / math.sqrt(32 * ROWS * LANES)
    any_ = pl.BlockSpec(memory_space=pl.ANY)
    vmem = pl.BlockSpec(memory_space=pltpu.VMEM)
    smem = pl.BlockSpec(memory_space=pltpu.SMEM)
    dma = pltpu.SemaphoreType.DMA
    gram, direct_modes, adjoint_modes = pl.pallas_call(
        functools.partial(kernel, weight),
        out_shape=(
            jax.ShapeDtypeStruct((128, 32), F32),
            jax.ShapeDtypeStruct((64, 2, LANES), F32),
            jax.ShapeDtypeStruct((64, 2, LANES), F32),
        ),
        in_specs=[any_, any_, any_, smem, smem, smem, any_, any_, vmem],
        out_specs=(vmem, vmem, vmem),
        scratch_shapes=[
            pltpu.VMEM((2, 2, PLANES, PART, ROWS, LANES), BF16),
            pltpu.VMEM((PLANES, ROWS, LANES), F32),
            pltpu.VMEM((LEVELS, PLANES, ROWS, LANES), F32),
            pltpu.VMEM((LEVELS, PLANES, ROWS, LANES), F32),
            pltpu.VMEM((2 * ROWS * PART, LANES), F32),
            pltpu.VMEM((4, 4, 8, PART, LANES), BF16),
            pltpu.VMEM((8, 2, 8, PART, LANES), BF16),
            pltpu.VMEM((4, 2, 2, 8, PART, LANES), BF16),
            pltpu.VMEM((16, 128, 128), BF16),
            pltpu.VMEM((16, 128, 128), BF16),
            pltpu.VMEM((128, 128), F32),
            pltpu.VMEM((4, 32, 128), F32),
            pltpu.VMEM((4, 32, 128), F32),
            pltpu.VMEM((2, 2, 64, LANES), F32),
            pltpu.VMEM((2, 2, 64, LANES), F32),
            pltpu.VMEM((4, 128, 64), F32),
            pltpu.VMEM((8, 2, PART, 64), F32),
            dma((4, 6)), dma((4, 6)),
            dma((6,)), dma((6,)),
            dma((7,)),
            dma((4, 8)), dma((4, 8)),
            dma((16,)), dma((16,)),
            dma((4,)), dma((4,)),
            dma((2,)), dma((2,)),
        ],
        compiler_params=pltpu.CompilerParams(
            collective_id=0, has_side_effects=True, vmem_limit_bytes=48 * 1024 * 1024
        ),
        name="window",
    )(
        forcing_direct.reshape(128, ROWS, LANES),
        forcing_adjoint.reshape(128, ROWS, LANES),
        conductance.reshape(ROWS, LANES),
        shift_table,
        freq_direct,
        freq_adjoint,
        left_factors.reshape(8, 128, 64),
        right_factors.reshape(8, 2, 2, PART, 64),
        singular_values.reshape(1, 64),
    )
    return (
        gram,
        direct_modes.reshape(64, 1, 2, LANES),
        adjoint_modes.reshape(64, 1, 2, LANES),
    )


def solution(mesh):
    placed = (
        P("snap", "space", None, None),
        P("snap", "space", None, None),
        P("space", None, None),
        P(),
        P("snap"),
        P("snap"),
        P(),
        P(),
        P(),
    )
    return jax.shard_map(
        per_device,
        mesh=mesh,
        in_specs=placed,
        out_specs=(
            P("snap", "space"),
            P(None, "space", "snap", None),
            P(None, "space", "snap", None),
        ),
        check_vma=False,
    )
```

time: 1640 us -> 75.5 us (0.05)
  the two profiles are of different devices: /device:TPU:32 before, /device:TPU:8 now
where the time goes in v1:
time: 75.5 us; the launch traced here: 75.3 us
  Pallas kernels  70.5 us (93%)
  local copies, waits for them, and re-layouts  4.14 us (5%)
    pallas_call x1, Pallas kernels, per_device(): pl.pallas_call(functools.partial(kernel, weight), out_shape=(jax.ShapeDty...  70.5 us
    unnamed x21, local copies, waits for them, and re-layouts  4.14 us

profile of v1, /device:TPU:8, one launch (start us, length us, event | category | flops | bytes accessed | tf_op | source)
XLA Modules:
  0.0 75.3 jit_solution(3955672678969987215)
XLA Ops:
  0.6 0.0 copy-start.7
  0.6 0.0 copy-start.1
  0.7 1.2 %copy.12 = f32[1024,64]{1,0:T(8,128)S(1)} copy(f32[1024,64]{0,1:T(8,128)} %param.15) | data formatting | bytes 524288 | tf_op args[6]
  1.9 0.0 copy-start
  1.9 0.0 copy-done.7
  1.9 0.0 copy-start.2
  1.9 0.0 copy-start.6
  1.9 0.2 copy.13
  2.1 0.0 copy-start.3
  2.1 0.0 copy-start.4
  2.1 0.0 copy-start.5
  2.2 0.0 copy-done.1
  2.2 0.8 copy-done
  2.9 0.0 copy-done.2
  2.9 0.0 copy-done.6
  2.9 0.0 copy-done.3
  2.9 0.0 copy-done.4
  2.9 0.0 copy-done.5
  2.9 70.5 %window.1 = (f32[128,32]{1,0:T(8,128)S(1)}, f32[64,2,128]{2,1,0:T(2,128)S(1)}, f32[64,2,128]{2,1,0:T(2,128)S(1)}) custom-call(bf16[128,16,128]{2,1,0:T(8,128)(2,1)S(1)} %bitcast.14, bf16[128,16,128]{2,1,0:T(8,128)(2,1)S(1)} %bitcast.15, f32[16,128]{1,0:T(8,128)S(1)} %bitcast.18, f32[16]{0:T(128)S(1)} %copy-done.3, s32[128]{0:T(128)S(1)} %copy-done.4, ...), custom_call_target="tpu_custom_call" | custom-call | tf_op jit(solution)/shard_map/window/pallas_call | solution.py:429
  73.4 0.7 copy.14
  74.1 0.6 copy.19
  74.7 0.6 copy.20
Async XLA Ops:
  0.6 1.3 %copy-start.7 = (f32[1024,64]{0,1:T(8,128)S(1)}, f32[1024,64]{0,1:T(8,128)}, u32[]{:S(2)}) copy-start(f32[1024,64]{0,1:T(8,128)} %param.16) | copy-start | bytes 786436
  0.6 1.5 %copy-start.1 = (bf16[128,1,16,128]{3,2,1,0:T(8,128)(2,1)S(1)}, bf16[128,1,16,128]{3,2,1,0:T(8,128)(2,1)}, u32[]{:S(2)}) copy-start(bf16[128,1,16,128]{3,2,1,0:T(8,128)(2,1)} %param.10) | copy-start | bytes 1572868
  1.9 1.0 %copy-start = (bf16[128,1,16,128]{3,2,1,0:T(8,128)(2,1)S(1)}, bf16[128,1,16,128]{3,2,1,0:T(8,128)(2,1)}, u32[]{:S(2)}) copy-start(bf16[128,1,16,128]{3,2,1,0:T(8,128)(2,1)} %param.9) | copy-start | bytes 1572868
  1.9 1.0 %copy-start.2 = (f32[1,16,128]{2,1,0:T(8,128)S(1)}, f32[1,16,128]{2,1,0:T(8,128)}, u32[]{:S(2)}) copy-start(f32[1,16,128]{2,1,0:T(8,128)} %param.11) | copy-start | bytes 24580
  1.9 1.0 %copy-start.6 = (f32[64]{0:T(128)S(1)}, f32[64]{0:T(128)}, u32[]{:S(2)}) copy-start(f32[64]{0:T(128)} %param.17) | copy-start | bytes 772
  2.1 0.8 %copy-start.3 = (f32[16]{0:T(128)S(1)}, f32[16]{0:T(128)}, u32[]{:S(2)}) copy-start(f32[16]{0:T(128)} %table.1) | copy-start | bytes 196
  2.1 0.8 %copy-start.4 = (s32[128]{0:T(128)S(1)}, s32[128]{0:T(128)}, u32[]{:S(2)}) copy-start(s32[128]{0:T(128)} %freq_d.1) | copy-start | bytes 1540
  2.1 0.8 %copy-start.5 = (s32[128]{0:T(128)S(1)}, s32[128]{0:T(128)}, u32[]{:S(2)}) copy-start(s32[128]{0:T(128)} %freq_a.1) | copy-start | bytes 1540

commit v2 on v1

--- a/solution.py
+++ b/solution.py
@@ -17,14 +17,15 @@
 PLANES = 6
 PART = 32
 LEVELS = 16
+UNROLL = 4
 
 
 def contract_last(a, b):
     return lax.dot_general(a, b, (((1,), (1,)), ((), ())), preferred_element_type=F32)
 
 
-def contract_first(a, b):
-    return lax.dot_general(a, b, (((0,), (0,)), ((), ())), preferred_element_type=F32)
+def product(a, b):
+    return lax.dot_general(a, b, (((1,), (0,)), ((), ())), preferred_element_type=F32)
 
 
 def kernel(
@@ -32,7 +33,7 @@
     fd, fa, cond, table, freq_d, freq_a, left, right, sing,
     gram_o, dm_o, am_o,
     field, chalo, rtab, crtab, turn, outbox, dirbox, adjbox,
-    psend, precv, gsum, bsend, brecv, mpart, mrecv, lbuf, rbuf,
+    psend, precv, gsum, bsend, brecv, mpart, mrecv, lbuf, rbuf, rscaled,
     halo_s, halo_r, cond_s, cond_r, load_s, post_s, post_r, sa_s, sa_r, sb_s, sb_r, md_s, md_r,
 ):
     s = lax.axis_index("space")
@@ -118,8 +119,8 @@
     for c in range(4):
         to_neighbours(lambda dj, half: halo_copy(c, dj, half).start())
         halo_own(c).start()
-    lcopy = pltpu.make_async_copy(left.at[pl.ds(zh * 4, 4)], lbuf, load_s.at[4])
-    rcopy = pltpu.make_async_copy(right.at[:, :, h], rbuf, load_s.at[5])
+    lcopy = pltpu.make_async_copy(left.at[:, pl.ds(pl.multiple_of(zh * 512, 512), 512)], lbuf, load_s.at[4])
+    rcopy = pltpu.make_async_copy(right, rbuf, load_s.at[5])
     ccopy = pltpu.make_async_copy(cond, chalo.at[2 + h], load_s.at[6])
     lcopy.start()
     rcopy.start()
@@ -220,7 +221,7 @@
                 turn[pl.ds(k * ROWS * PART + n, ROWS, stride=PART), :] = a2[k]
             return carry
 
-        lax.fori_loop(0, PART, one, 0)
+        lax.fori_loop(0, PART, one, 0, unroll=UNROLL)
 
     def pack(c):
         for k in range(2):
@@ -278,21 +279,27 @@
 
     lcopy.wait()
     rcopy.wait()
-    inv_root = 1.0 / jnp.sqrt(sing[...])
-    left_s = (lbuf[...].reshape(512, 64) * inv_root).astype(BF16)
-    right_s = (rbuf[...].reshape(512, 64) * inv_root).astype(BF16)
-
-    def arrived(c):
-        for dz, dx in far_first:
+    inv_root = jnp.broadcast_to(1.0 / jnp.sqrt(sing[...]), (64, 64))
+    across = lax.broadcasted_iota(jnp.int32, (64, 64), 1)
+    along = lax.broadcasted_iota(jnp.int32, (64, 64), 0)
+    inv_root = jnp.sum(jnp.where(across == along, inv_root, 0.0), axis=1, keepdims=True)
+    left_s = (lbuf[...] * inv_root).astype(BF16)
+    scaled = rbuf[...] * inv_root
+    scaled = jnp.where(h == 1, pltpu.roll(scaled, 1024 - PART, 1), scaled)
+    for zz in range(2):
+        rscaled[zz] = jnp.concatenate(
+            [scaled[:, q * 64 : q * 64 + PART] for q in range(zz * 8, zz * 8 + 8)], axis=1
+        ).astype(BF16)
+
+    def arrived(c, dz):
+        for dx in (2, 1, 3, 0):
             if dz == 0 and dx == 0:
                 post(c, 0, 0).wait()
             else:
                 post_arrival(c, dz, dx)
 
-    for c in range(4):
-        arrived(c)
-
-    def adj_rows(xx):
+    def adj_rows(dx):
+        xx = (x + dx) % 4
         pieces = [
             jnp.concatenate([adjbox[xx, hh, part, rho] for rho in range(8)], axis=1)
             for hh in range(2)
@@ -300,37 +307,51 @@
         ]
         return jnp.concatenate(pieces, axis=0)
 
-    adj_all = [adj_rows((x + dx) % 4) for dx in range(4)]
-
-    def sa_copy(dy, dx):
+    def dir_rows(zz, yy, part):
+        pieces = [
+            jnp.concatenate(
+                [dirbox[4 * zz + 2 * t + yy // 2, part, rho] for rho in range(8)], axis=1
+            )
+            for t in range(2)
+        ]
+        return jnp.concatenate(pieces, axis=0)
+
+    def sa_copy(half, dy, dx):
         return pltpu.make_async_remote_copy(
-            src_ref=psend.at[dy * 4 + dx],
-            dst_ref=precv.at[dy * 4 + dx],
-            send_sem=sa_s.at[dy * 4 + dx],
-            recv_sem=sa_r.at[dy * 4 + dx],
+            src_ref=psend.at[half, dy * 4 + dx],
+            dst_ref=precv.at[half, dy * 4 + dx],
+            send_sem=sa_s.at[half, dy * 4 + dx],
+            recv_sem=sa_r.at[half, dy * 4 + dx],
             device_id=dev(2 * (zl * 4 + (y + dy) % 4) + h, zh * 4 + (x + dx) % 4),
             device_id_type=MESH,
         )
 
-    for dy in (2, 1, 3, 0):
-        yy = (y + dy) % 4
-        pieces = [
-            jnp.concatenate([dirbox[2 * zz + yy // 2, yy % 2, rho] for rho in range(8)], axis=1)
-            for zz in range(4)
-        ]
-        dir_y = jnp.concatenate(pieces, axis=0)
-        for dx in (2, 1, 3, 0):
-            block = contract_last(dir_y, adj_all[dx])
-            if dy == 0 and dx == 0:
-                gsum[...] = block
+    def ship(half, dy, dx, block):
+        psend[half, dy * 4 + dx] = block.astype(BF16)
+        sa_copy(half, dy, dx).start()
+
+    arrived(0, 0)
+    arrived(1, 0)
+    arrived(2, 1)
+    arrived(2, 0)
+    arrived(3, 1)
+    arrived(3, 0)
+    turns = (2, 1, 3, 0)
+    dir_own = jnp.concatenate(
+        [dir_rows(zh, (y + dy) % 4, (y + dy) % 2) for dy in turns], axis=0
+    )
+    for dx in turns:
+        block = contract_last(dir_own, adj_rows(dx))
+        for i, dy in enumerate(turns):
+            if dx == 0 and dy == 0:
+                gsum[0] = block[64 * i : 64 * i + 64]
             else:
-                psend[dy * 4 + dx] = block.astype(BF16)
-                sa_copy(dy, dx).start()
-
-    def dir_cells(k, t):
+                ship(0, dy, dx, block[64 * i : 64 * i + 64])
+
+    def dir_cells(zz, k, t):
         rho = k * 4 + 2 * zh + t
         return jnp.concatenate(
-            [dirbox[pp, part, rho] for pp in range(8) for part in range(2)], axis=0
+            [dirbox[4 * zz + i, part, rho] for i in range(4) for part in range(2)], axis=0
         )
 
     def adj_cells(zz, t):
@@ -339,10 +360,6 @@
             [adjbox[xx, hh, part, rho] for xx in range(4) for hh in range(2) for part in range(2)],
             axis=0,
         )
-
-    for t in range(2):
-        mpart[0, t] = contract_first(right_s, dir_cells(1 - h, t))
-        mpart[1, t] = contract_first(left_s, adj_cells(1 - zh, t))
 
     def md_copy(fam):
         target = dev(2 * j + 1 - h, p) if fam == 0 else dev(s, (1 - zh) * 4 + x)
@@ -355,20 +372,33 @@
             device_id_type=MESH,
         )
 
-    for fam in range(2):
-        md_copy(fam).start()
-    own_d = [contract_first(right_s, dir_cells(h, t)) for t in range(2)]
-    own_a = [contract_first(left_s, adj_cells(zh, t)) for t in range(2)]
-
-    for dy in (1, 3, 2, 0):
-        for dx in (1, 3, 2, 0):
-            if dy or dx:
-                sa_copy(dy, dx).wait_recv()
-    total = gsum[...]
-    for i in range(1, 16):
-        total = total + precv[i].astype(F32)
-    for zz in range(4):
-        bsend[zz] = total[zz * 32 : zz * 32 + 32]
+    for t in range(2):
+        mpart[1, t] = product(left_s, adj_cells(1 - zh, t))
+    md_copy(1).start()
+    for t in range(2):
+        mpart[0, t] = product(rscaled[zh], dir_cells(zh, 1 - h, t))
+        dm_o[:, t, :] = product(rscaled[zh], dir_cells(zh, h, t))
+        am_o[:, t, :] = product(left_s, adj_cells(zh, t))
+
+    def other_half(part):
+        first = dir_rows(1 - zh, part, part)
+        second = dir_rows(1 - zh, 2 + part, part)
+        rows = jnp.concatenate([first, second], axis=0)
+        for dx in turns:
+            block = contract_last(rows, adj_rows(dx))
+            for i in range(2):
+                piece = block[64 * i : 64 * i + 64]
+                dy = (2 * i + part - y + 4) % 4
+                if dx:
+                    ship(1, dy, dx, piece)
+                else:
+                    @pl.when(dy == 0)
+                    def _():
+                        gsum[1] = piece
+
+                    @pl.when(dy != 0)
+                    def _():
+                        ship(1, dy, dx, piece)
 
     def sb_copy(dz):
         return pltpu.make_async_remote_copy(
@@ -380,19 +410,42 @@
             device_id_type=MESH,
         )
 
-    for dz in (2, 1, 3):
-        sb_copy(dz).start()
-
-    for fam in range(2):
-        md_copy(fam).wait_recv()
+    def add_up(half):
+        for dy in (1, 3, 2, 0):
+            for dx in (1, 3, 2, 0):
+                if dy or dx:
+                    sa_copy(half, dy, dx).wait_recv()
+        total = gsum[half]
+        for i in range(1, 16):
+            total = total + precv[half, i].astype(F32)
+        zz = zh if half == 0 else 1 - zh
+        for t in range(2):
+            bsend[2 * zz + t] = total[t * 32 : t * 32 + 32]
+        for dz in (2, 1, 3):
+            @pl.when(((zl + dz) % 4) // 2 == zz)
+            def _():
+                sb_copy(dz).start()
+
+    arrived(0, 1)
+    other_half(0)
+    add_up(0)
+    arrived(1, 1)
+    other_half(1)
     for t in range(2):
-        dm_o[:, t, :] = own_d[t] + mrecv[0, t]
-        am_o[:, t, :] = own_a[t] + mrecv[1, t]
-
+        mpart[0, t] = mpart[0, t] + product(rscaled[1 - zh], dir_cells(1 - zh, 1 - h, t))
+    md_copy(0).start()
+    for t in range(2):
+        dm_o[:, t, :] = dm_o[:, t, :] + product(rscaled[1 - zh], dir_cells(1 - zh, h, t))
+    md_copy(1).wait_recv()
+    for t in range(2):
+        am_o[:, t, :] = am_o[:, t, :] + mrecv[1, t]
+    add_up(1)
+    md_copy(0).wait_recv()
+    for t in range(2):
+        dm_o[:, t, :] = dm_o[:, t, :] + mrecv[0, t]
     for dz in (1, 3, 2):
         sb_copy(dz).wait_recv()
-    mine = bsend[zl] + brecv[1] + brecv[2] + brecv[3]
-    gram_o[...] = (mine * weight).T
+    gram_o[...] = (bsend[zl] + brecv[1] + brecv[2] + brecv[3]) * weight
 
     to_neighbours(lambda dj, half: cond_copy(dj, half).wait_send())
     for c in range(4):
@@ -403,7 +456,8 @@
     for dy in range(4):
         for dx in range(4):
             if dy or dx:
-                sa_copy(dy, dx).wait_send()
+                sa_copy(0, dy, dx).wait_send()
+                sa_copy(1, dy, dx).wait_send()
     for dz in range(1, 4):
         sb_copy(dz).wait_send()
     for fam in range(2):
@@ -422,14 +476,14 @@
     singular_values,
 ):
     weight = 1.0 / math.sqrt(32 * ROWS * LANES)
-    any_ = pl.BlockSpec(memory_space=pl.ANY)
+    any_ = pl.BlockSpec(memory_space=pltpu.HBM)
     vmem = pl.BlockSpec(memory_space=pltpu.VMEM)
     smem = pl.BlockSpec(memory_space=pltpu.SMEM)
     dma = pltpu.SemaphoreType.DMA
     gram, direct_modes, adjoint_modes = pl.pallas_call(
         functools.partial(kernel, weight),
         out_shape=(
-            jax.ShapeDtypeStruct((128, 32), F32),
+            jax.ShapeDtypeStruct((32, 128), F32),
             jax.ShapeDtypeStruct((64, 2, LANES), F32),
             jax.ShapeDtypeStruct((64, 2, LANES), F32),
         ),
@@ -444,25 +498,26 @@
             pltpu.VMEM((4, 4, 8, PART, LANES), BF16),
             pltpu.VMEM((8, 2, 8, PART, LANES), BF16),
             pltpu.VMEM((4, 2, 2, 8, PART, LANES), BF16),
-            pltpu.VMEM((16, 128, 128), BF16),
-            pltpu.VMEM((16, 128, 128), BF16),
-            pltpu.VMEM((128, 128), F32),
+            pltpu.VMEM((2, 16, 64, 128), BF16),
+            pltpu.VMEM((2, 16, 64, 128), BF16),
+            pltpu.VMEM((2, 64, 128), F32),
             pltpu.VMEM((4, 32, 128), F32),
             pltpu.VMEM((4, 32, 128), F32),
             pltpu.VMEM((2, 2, 64, LANES), F32),
             pltpu.VMEM((2, 2, 64, LANES), F32),
-            pltpu.VMEM((4, 128, 64), F32),
-            pltpu.VMEM((8, 2, PART, 64), F32),
+            pltpu.VMEM((64, 512), F32),
+            pltpu.VMEM((64, 1024), F32),
+            pltpu.VMEM((2, 64, 256), BF16),
             dma((4, 6)), dma((4, 6)),
             dma((6,)), dma((6,)),
             dma((7,)),
             dma((4, 8)), dma((4, 8)),
-            dma((16,)), dma((16,)),
+            dma((2, 16)), dma((2, 16)),
             dma((4,)), dma((4,)),
             dma((2,)), dma((2,)),
         ],
         compiler_params=pltpu.CompilerParams(
-            collective_id=0, has_side_effects=True, vmem_limit_bytes=48 * 1024 * 1024
+            collective_id=0, has_side_effects=True, vmem_limit_bytes=63 * 1024 * 1024
         ),
         name="window",
     )(
@@ -472,12 +527,12 @@
         shift_table,
         freq_direct,
         freq_adjoint,
-        left_factors.reshape(8, 128, 64),
-        right_factors.reshape(8, 2, 2, PART, 64),
+        left_factors.T,
+        right_factors.T,
         singular_values.reshape(1, 64),
     )
     return (
-        gram,
+        gram.T,
         direct_modes.reshape(64, 1, 2, LANES),
         adjoint_modes.reshape(64, 1, 2, LANES),
     )

time: 75.5 us -> 74.2 us (0.983)
  the two profiles are of different devices: /device:TPU:8 before, /device:TPU:72 now
where the time goes in v2:
time: 74.2 us; the launch traced here: 73.9 us
  Pallas kernels  69.8 us (94%)
  local copies, waits for them, and re-layouts  3.46 us (5%)
    pallas_call x1, Pallas kernels, per_device(): pl.pallas_call(functools.partial(kernel, weight), out_shape=(jax.ShapeDty...  69.8 us
    unnamed x5, local copies, waits for them, and re-layouts  3.46 us

profile of v2, /device:TPU:72, one launch (start us, length us, event | category | flops | bytes accessed | tf_op | source)
XLA Modules:
  0.0 73.9 jit_solution(10701443435283794182)
XLA Ops:
  0.6 69.8 %window.1 = (f32[32,128]{1,0:T(8,128)}, f32[64,2,128]{2,1,0:T(2,128)}, f32[64,2,128]{2,1,0:T(2,128)}) custom-call(bf16[128,16,128]{2,1,0:T(8,128)(2,1)} %bitcast.13, bf16[128,16,128]{2,1,0:T(8,128)(2,1)} %bitcast.14, f32[16,128]{1,0:T(8,128)} %bitcast.20, f32[16]{0:T(128)} %table.1, s32[128]{0:T(128)} %freq_d.1, s32[128]{0:T(128)} %freq_a.1, ...), custom_call_target="tpu_custom_call" | custom-call | tf_op jit(solution)/shard_map/window/pallas_call | solution.py:483
  70.5 1.3 %copy.17 = f32[128,32]{0,1:T(8,128)} copy(f32[128,32]{0,1:T(8,128)} %bitcast.19) | data formatting | bytes 32768
  71.8 0.0 copy-start
  71.8 1.5 %copy.18 = f32[64,1,2,128]{3,2,1,0:T(2,128)} copy(f32[64,1,2,128]{3,2,1,0:T(2,128)} %bitcast.18) | data formatting | bytes 131072
  73.3 0.0 copy-done
  73.3 0.6 copy.19
Async XLA Ops:
  71.8 1.5 %copy-start = (f32[64,2,128]{2,1,0:T(2,128)S(1)}, f32[64,2,128]{2,1,0:T(2,128)}, u32[]{:S(2)}) copy-start(f32[64,2,128]{2,1,0:T(2,128)} %get-tuple-element.8) | copy-start | bytes 196612

commit v3 on v2

--- a/solution.py
+++ b/solution.py
@@ -475,6 +475,7 @@
     right_factors,
     singular_values,
 ):
+    hold = lambda v: pltpu.with_memory_space_constraint(v, pltpu.HBM)
     weight = 1.0 / math.sqrt(32 * ROWS * LANES)
     any_ = pl.BlockSpec(memory_space=pltpu.HBM)
     vmem = pl.BlockSpec(memory_space=pltpu.VMEM)
@@ -517,19 +518,19 @@
             dma((2,)), dma((2,)),
         ],
         compiler_params=pltpu.CompilerParams(
-            collective_id=0, has_side_effects=True, vmem_limit_bytes=63 * 1024 * 1024
+            collective_id=0, has_side_effects=True, vmem_limit_bytes=50 * 1024 * 1024
         ),
         name="window",
     )(
-        forcing_direct.reshape(128, ROWS, LANES),
-        forcing_adjoint.reshape(128, ROWS, LANES),
-        conductance.reshape(ROWS, LANES),
-        shift_table,
-        freq_direct,
-        freq_adjoint,
-        left_factors.T,
-        right_factors.T,
-        singular_values.reshape(1, 64),
+        hold(forcing_direct.reshape(128, ROWS, LANES)),
+        hold(forcing_adjoint.reshape(128, ROWS, LANES)),
+        hold(conductance.reshape(ROWS, LANES)),
+        hold(shift_table),
+        hold(freq_direct),
+        hold(freq_adjoint),
+        hold(left_factors.T),
+        hold(right_factors.T),
+        hold(singular_values.reshape(1, 64)),
     )
     return (
         gram.T,

time: 74.2 us -> 71.8 us (0.968)
  local copies, waits for them, and re-layouts: 3.46 us -> 1.87 us
    unnamed x5 -> x3, local copies, waits for them, and re-layouts: 3.46 us -> 1.87 us
where the time goes in v3:
time: 71.8 us; the launch traced here: 71.7 us
  Pallas kernels  69.2 us (96%)
  local copies, waits for them, and re-layouts  1.87 us (3%)
    pallas_call x1, Pallas kernels, per_device(): pl.pallas_call(functools.partial(kernel, weight), out_shape=(jax.ShapeDty...  69.2 us
    unnamed x3, local copies, waits for them, and re-layouts  1.87 us

profile of v3, /device:TPU:72, one launch (start us, length us, event | category | flops | bytes accessed | tf_op | source)
XLA Modules:
  0.0 71.7 jit_solution(2573730155363877352)
XLA Ops:
  0.6 69.2 %window.1 = (f32[32,128]{1,0:T(8,128)S(1)}, f32[64,2,128]{2,1,0:T(2,128)S(1)}, f32[64,2,128]{2,1,0:T(2,128)S(1)}) custom-call(bf16[128,16,128]{2,1,0:T(8,128)(2,1)} %bitcast.16, bf16[128,16,128]{2,1,0:T(8,128)(2,1)} %bitcast.17, f32[16,128]{1,0:T(8,128)} %bitcast.20, f32[16]{0:T(128)} %table.1, s32[128]{0:T(128)} %freq_d.1, s32[128]{0:T(128)} %freq_a.1, ...), custom_call_target="tpu_custom_call" | custom-call | tf_op jit(solution)/shard_map/window/pallas_call | solution.py:484
  69.8 0.6 copy.17
  70.4 0.6 copy.18
  71.1 0.6 copy.19

commit v4 on v3

--- a/solution.py
+++ b/solution.py
@@ -17,7 +17,7 @@
 PLANES = 6
 PART = 32
 LEVELS = 16
-UNROLL = 4
+UNROLL = 2
 
 
 def contract_last(a, b):
@@ -268,7 +268,7 @@
             device_id_type=MESH,
         ).wait_recv()
 
-    far_first = [(dz, dx) for dz in (1, 0) for dx in (2, 1, 3, 0)]
+    far_first = [(dz, dx) for dz in (1, 0) for dx in (3, 2, 1, 0)]
     for c in range(4):
         halo_own(c).wait()
         from_neighbours(halo_arrival(c))

time: 71.8 us -> 71.3 us (level)
  no operation moved by 1% of the time
where the time goes in v4:
time: 71.3 us; the launch traced here: 71.2 us
  Pallas kernels  68.6 us (96%)
  local copies, waits for them, and re-layouts  1.87 us (3%)
    pallas_call x1, Pallas kernels, per_device(): pl.pallas_call(functools.partial(kernel, weight), out_shape=(jax.ShapeDty...  68.6 us
    unnamed x3, local copies, waits for them, and re-layouts  1.87 us

profile of v4, /device:TPU:72, one launch (start us, length us, event | category | flops | bytes accessed | tf_op | source)
XLA Modules:
  0.0 71.2 jit_solution(13303115651298432388)
XLA Ops:
  0.6 68.6 %window.1 = (f32[32,128]{1,0:T(8,128)S(1)}, f32[64,2,128]{2,1,0:T(2,128)S(1)}, f32[64,2,128]{2,1,0:T(2,128)S(1)}) custom-call(bf16[128,16,128]{2,1,0:T(8,128)(2,1)} %bitcast.16, bf16[128,16,128]{2,1,0:T(8,128)(2,1)} %bitcast.17, f32[16,128]{1,0:T(8,128)} %bitcast.20, f32[16]{0:T(128)} %table.1, s32[128]{0:T(128)} %freq_d.1, s32[128]{0:T(128)} %freq_a.1, ...), custom_call_target="tpu_custom_call" | custom-call | tf_op jit(solution)/shard_map/window/pallas_call | solution.py:484
  69.3 0.6 copy.17
  69.9 0.6 copy.18
  70.5 0.6 copy.19

commit v5 on v4

--- a/solution.py
+++ b/solution.py
@@ -426,9 +426,9 @@
             def _():
                 sb_copy(dz).start()
 
+    add_up(0)
     arrived(0, 1)
     other_half(0)
-    add_up(0)
     arrived(1, 1)
     other_half(1)
     for t in range(2):

time: 71.3 us -> 71.3 us (level)
  no operation moved by 1% of the time
where the time goes in v5:
time: 71.3 us; the launch traced here: 71.2 us
  Pallas kernels  68.6 us (96%)
  local copies, waits for them, and re-layouts  1.87 us (3%)
    pallas_call x1, Pallas kernels, per_device(): pl.pallas_call(functools.partial(kernel, weight), out_shape=(jax.ShapeDty...  68.6 us
    unnamed x3, local copies, waits for them, and re-layouts  1.87 us

profile of v5, /device:TPU:72, one launch (start us, length us, event | category | flops | bytes accessed | tf_op | source)
XLA Modules:
  0.0 71.2 jit_solution(6122125855156280811)
XLA Ops:
  0.6 68.6 %window.1 = (f32[32,128]{1,0:T(8,128)S(1)}, f32[64,2,128]{2,1,0:T(2,128)S(1)}, f32[64,2,128]{2,1,0:T(2,128)S(1)}) custom-call(bf16[128,16,128]{2,1,0:T(8,128)(2,1)} %bitcast.16, bf16[128,16,128]{2,1,0:T(8,128)(2,1)} %bitcast.17, f32[16,128]{1,0:T(8,128)} %bitcast.20, f32[16]{0:T(128)} %table.1, s32[128]{0:T(128)} %freq_d.1, s32[128]{0:T(128)} %freq_a.1, ...), custom_call_target="tpu_custom_call" | custom-call | tf_op jit(solution)/shard_map/window/pallas_call | solution.py:484
  69.3 0.6 copy.17
  69.9 0.6 copy.18
  70.5 0.6 copy.19
